TPU v7x, 256 devices: a whole 4x4x8 slice. The times are simulated.
256 devices in a mesh: row: 2 (over core), col: 64 (over z, y, x_hi), layer: 2 (over x_lo).
Axes of the slice: x: 4 (x_hi: 2, x_lo: 2; x = x_hi * 2 + x_lo), y: 4, z: 8, core: 2. Of those that a mesh axis runs over, the one named last changes fastest.
Arguments:
- flow_cols: int32 [16, 2, 64], P('row', 'layer', 'col'), may hold values from 0 to 64, as said below
- flow_vals: bfloat16 [16, 2, 64, 128, 128], P('row', 'layer', 'col'), may hold values from -22 to 22
- window_flow: bfloat16 [2, 8192, 32768], P('layer', 'row', 'col'), may hold values from -0.1403165 to 0.1403165
Outputs:
- flow_next: float32 [2048, 32768], P(('row', 'layer'), 'col')
Inputs may be any that keep to these rules, and one draw needn't show every extreme that they name: `flow_cols`: an entry 64 marks an empty slot; the live entries of one block row and layer are distinct; every block row and layer has at least one live slot, and some block row and layer has all 64 slots live.
All inputs are finite; a program needn't handle non-finite values.
Results may differ from a plain program's by a relative error of at most 0.0003.
Values may be sent and summed in bfloat16 or wider, within the bound.
A program may use at most 128 MiB of HBM per device.

v0:
```python
import jax
import jax.numpy as jnp
from jax import lax
from jax.sharding import PartitionSpec as P


def body(flow_cols, flow_vals, window_flow):
    window_panel = lax.all_gather(window_flow[0], "row", axis=0, tiled=True)
    block_size = flow_vals.shape[-1]
    block_count = window_panel.shape[0] // block_size
    row_blocks = flow_vals.shape[0]
    all_cols, all_vals = (
        lax.all_gather(flow_cols, "col", axis=2, tiled=True),
        lax.all_gather(flow_vals, "col", axis=2, tiled=True),
    )
    slot_cols = all_cols[:, 0, :]
    slot_vals = all_vals[:, 0]
    column_ids = jnp.arange(block_count, dtype=jnp.int32)
    one_hot = (slot_cols[:, :, None] == column_ids[None, None, :]).astype(jnp.bfloat16)
    dense_row = jnp.einsum(
        "isab,isk->iakb", slot_vals, one_hot, preferred_element_type=jnp.bfloat16
    )
    dense_row = dense_row.reshape(row_blocks * block_size, block_count * block_size)
    expanded = jnp.dot(dense_row, window_panel, preferred_element_type=jnp.float32)
    total_rows = row_blocks * block_size * lax.axis_size("row")
    summed = lax.psum(expanded, "layer")
    all_squares = summed * summed
    column_sums = lax.psum(jnp.sum(all_squares, axis=0), "row")
    share_rows = summed.shape[0] // lax.axis_size("layer")
    squares = lax.dynamic_slice_in_dim(
        all_squares, lax.axis_index("layer") * share_rows, share_rows, 0
    )
    return squares / (column_sums / total_rows + 1e-06)


def solution(mesh):
    placed = (
        P("row", "layer", "col"),
        P("row", "layer", "col", None, None),
        P("layer", "row", "col"),
    )
    return jax.shard_map(
        body, mesh=mesh, in_specs=placed, out_specs=P(("row", "layer"), "col"), check_vma=False
    )
```

profile of v0, /device:TPU:1, one launch (start us, length us, event | category | flops | bytes accessed | tf_op | source)
XLA Modules:
  0.0 361.2 jit_solution(3582234207168179350)
XLA Ops:
  6.5 0.0 all-gather.4.cloned.1.call-start
  6.5 0.7 all-gather.4.cloned.1.call-update
  7.3 0.0 all-gather.6.cloned.1.call-start
  7.3 0.7 all-gather.6.cloned.1.call-update
  8.0 0.0 all-reduce.2.cloned.1.call-start
  8.1 156.8 %all_gather.9 = s32[8,1,64]{0,1,2:T(1,128)S(1)} all-gather(s32[8,1,1]{0,1,2:T(1,128)} %bitcast.23), channel_id=1, replica_groups=mesh['row'=2,'col'=64,'layer'=2] {'col'}, dimensions={2}, use_global_device_ids=true | all-gather | bytes 2080 | tf_op jit(solution)/shard_map/all_gather | solution.py:13
  164.9 0.1 copy.7
  165.0 58.9 %all-gather.4.cloned.1.call-done = bf16[8,1,64,128,128]{4,3,1,0,2:T(8,128)(2,1)} async-done(((bf16[8,1,1,128,128]{4,3,1,0,2:T(8,128)(2,1)}), bf16[8,1,64,128,128]{4,3,1,0,2:T(8,128)(2,1)}) %all-gather.4.cloned.1.call-update) | async-done | bytes 16777232 | tf_op jit(solution)/shard_map/all_gather | solution.py:14
  223.9 22.9 %fusion.3 = bf16[8,64,128,128]{3,1,2,0:T(8,128)(2,1)} fusion(bf16[8,1,64,128,128]{4,3,1,0,2:T(8,128)(2,1)} %all-gather.4.cloned.1.call-done, s32[8,64]{1,0:T(8,128)S(1)} %copy.7), kind=kOutput, calls=%fused_computation.3 | convolution fusion | flops 1073774592 | bytes 33556480 | tf_op jit(solution)/shard_map/isab,isk->iakb/dot_general | solution.py:20
  246.8 2.1 all-gather.6.cloned.1.call-done
  248.9 24.6 %fusion = f32[1024,512]{1,0:T(8,128)} fusion(bf16[128,8,64,128]{3,2,1,0:T(8,128)(2,1)} %bitcast.20, bf16[1,8192,512]{2,1,0:T(8,128)(2,1)} %all-gather.6.cloned.1.call-done), kind=kOutput, calls=%fused_computation | convolution fusion | flops 8589934592 | bytes 27262976 | tf_op jit(solution)/shard_map/dot_general | solution.py:24
  273.5 0.0 all-reduce.2.cloned.1.call-update
  273.5 75.3 %all-reduce.2.cloned.1.call-done = f32[1024,512]{1,0:T(8,128)} async-done(((f32[1024,512]{1,0:T(8,128)}), f32[1024,512]{1,0:T(8,128)}) %all-reduce.2.cloned.1.call-update) | async-done | bytes 2097168 | tf_op jit(solution)/shard_map/psum | solution.py:26
  348.8 1.9 multiply_reduce_fusion
  350.7 2.8 psum.15
  353.6 1.1 dynamic-slice_divide_fusion
  (1 shorter events, 0.0 us)
Async XLA Ops:
  6.5 217.4 %all-gather.4.cloned.1.call-start = ((), (), s32[]{:S(2)}) async-start(), calls=%async_computation | async-start | bytes 17039360 | tf_op jit(solution)/shard_map/all_gather | solution.py:14
  7.3 241.6 %all-gather.6.cloned.1.call-start = ((), (), s32[]{:S(2)}) async-start(), calls=%async_computation.2 | async-start | bytes 12582912 | tf_op jit(solution)/shard_map/all_gather | solution.py:8
  8.0 340.8 %all-reduce.2.cloned.1.call-start = ((), (), s32[]{:S(2)}) async-start(), calls=%async_computation.1 | async-start | bytes 4194304 | tf_op jit(solution)/shard_map/psum | solution.py:26
Sparse Core Ops, SparseCore 0:
  11.1 212.7 all-gather.3
  225.7 23.1 all-gather.5
  273.6 75.1 all-reduce.1
where the time goes:
time: 361 us
  blocking collectives  160 us (44%)
  waiting for transfers between devices  138 us (38%)
  matrix products  47.5 us (13%)
  between operations  13.1 us (4%)
    all_gather x1, blocking collectives, body(): lax.all_gather(flow_cols, 'col', axis=2, tiled=True)  157 us
    psum x1, waiting for transfers between devices, body(): summed = lax.psum(expanded, 'layer')  75.3 us
    all_gather x1, waiting for transfers between devices, body(): lax.all_gather(flow_vals, 'col', axis=2, tiled=True)  58.9 us
    dot_general x1, matrix products, body(): jnp.dot(dense_row, window_panel, preferred_element_type=jnp.float32)  24.6 us
    dot_general x1, matrix products, body(): jnp.einsum('isab,isk->iakb', slot_vals, one_hot, preferred_element_type=j...  22.9 us
  transfers between devices with their start and end apart: 3, of which 3 were waited for; matrix products, arithmetic and copies ran while one was open for 6% of the time, Pallas kernels for 0%

commit v1 on v0

--- a/solution.py
+++ b/solution.py
@@ -23,7 +23,7 @@
     dense_row = dense_row.reshape(row_blocks * block_size, block_count * block_size)
     expanded = jnp.dot(dense_row, window_panel, preferred_element_type=jnp.float32)
     total_rows = row_blocks * block_size * lax.axis_size("row")
-    summed = lax.psum(expanded, "layer")
+    summed = jnp.sum(lax.all_gather(expanded, "layer"), axis=0)
     all_squares = summed * summed
     column_sums = lax.psum(jnp.sum(all_squares, axis=0), "row")
     share_rows = summed.shape[0] // lax.axis_size("layer")

time: 361 us -> 352 us (0.975)
  waiting for transfers between devices: 138 us -> 125 us
  other arithmetic: 2.99 us -> 6.78 us
    psum x1 -> x0, waiting for transfers between devices: 75.3 us -> none  [body(): summed = lax.psum(expanded, 'layer')]
    all_gather x0 -> x1, waiting for transfers between devices: none -> 62.5 us  [body(): summed = jnp.sum(lax.all_gather(expanded, 'layer'), axis=0)]
  transfers between devices with their start and end apart: 3 -> 3, of which waited for: 3 -> 3; matrix products, arithmetic and copies ran while one was open for 6% -> 7% of each run, Pallas kernels for 0% -> 0%
where the time goes in v1:
time: 352 us
  blocking collectives  160 us (45%)
  waiting for transfers between devices  125 us (36%)
  matrix products  47.5 us (13%)
  between operations  13.1 us (4%)
  other arithmetic  6.78 us (2%)
    all_gather x1, blocking collectives, body(): lax.all_gather(flow_cols, 'col', axis=2, tiled=True)  157 us
    all_gather x1, waiting for transfers between devices, body(): summed = jnp.sum(lax.all_gather(expanded, 'layer'), axis=0)  62.5 us
    all_gather x1, waiting for transfers between devices, body(): lax.all_gather(flow_vals, 'col', axis=2, tiled=True)  58.9 us
    dot_general x1, matrix products, body(): jnp.dot(dense_row, window_panel, preferred_element_type=jnp.float32)  24.6 us
    dot_general x1, matrix products, body(): jnp.einsum('isab,isk->iakb', slot_vals, one_hot, preferred_element_type=j...  22.9 us
  transfers between devices with their start and end apart: 3, of which 3 were waited for; matrix products, arithmetic and copies ran while one was open for 7% of the time, Pallas kernels for 0%

profile of v1, /device:TPU:1, one launch (start us, length us, event | category | flops | bytes accessed | tf_op | source)
XLA Modules:
  0.0 352.1 jit_solution(15074289938609419050)
XLA Ops:
  6.5 0.0 all-gather.6.cloned.1.call-start
  6.5 0.7 all-gather.6.cloned.1.call-update
  7.3 0.0 all-gather.8.cloned.1.call-start
  7.3 0.7 all-gather.8.cloned.1.call-update
  8.0 0.0 all-gather.10.cloned.1.call-start
  8.1 156.8 %all_gather.15 = s32[8,1,64]{0,1,2:T(1,128)S(1)} all-gather(s32[8,1,1]{0,1,2:T(1,128)} %bitcast.25), channel_id=1, replica_groups=mesh['row'=2,'col'=64,'layer'=2] {'col'}, dimensions={2}, use_global_device_ids=true | all-gather | bytes 2080 | tf_op jit(solution)/shard_map/all_gather | solution.py:13
  164.9 0.1 copy.7
  165.0 58.9 %all-gather.6.cloned.1.call-done = bf16[8,1,64,128,128]{4,3,1,0,2:T(8,128)(2,1)} async-done(((bf16[8,1,1,128,128]{4,3,1,0,2:T(8,128)(2,1)}), bf16[8,1,64,128,128]{4,3,1,0,2:T(8,128)(2,1)}) %all-gather.6.cloned.1.call-update) | async-done | bytes 16777232 | tf_op jit(solution)/shard_map/all_gather | solution.py:14
  223.9 22.9 %fusion.3 = bf16[8,64,128,128]{3,1,2,0:T(8,128)(2,1)} fusion(bf16[8,1,64,128,128]{4,3,1,0,2:T(8,128)(2,1)} %all-gather.6.cloned.1.call-done, s32[8,64]{1,0:T(8,128)S(1)} %copy.7), kind=kOutput, calls=%fused_computation.3 | convolution fusion | flops 1073774592 | bytes 33556480 | tf_op jit(solution)/shard_map/isab,isk->iakb/dot_general | solution.py:20
  246.8 2.1 all-gather.8.cloned.1.call-done
  248.9 24.6 %fusion = f32[1024,512]{1,0:T(8,128)} fusion(bf16[128,8,64,128]{3,2,1,0:T(8,128)(2,1)} %bitcast.21, bf16[1,8192,512]{2,1,0:T(8,128)(2,1)} %all-gather.8.cloned.1.call-done), kind=kOutput, calls=%fused_computation | convolution fusion | flops 8589934592 | bytes 27262976 | tf_op jit(solution)/shard_map/dot_general | solution.py:24
  273.5 0.0 all-gather.10.cloned.1.call-update
  273.5 62.5 %all-gather.10.cloned.1.call-done = f32[2048,512]{1,0:T(8,128)} async-done(((f32[1024,512]{1,0:T(8,128)}), f32[2048,512]{1,0:T(8,128)}) %all-gather.10.cloned.1.call-update) | async-done | bytes 4194320 | tf_op jit(solution)/shard_map/all_gather | solution.py:26
  336.0 2.9 reduce_sum.18
  338.9 1.6 multiply_reduce_fusion
  340.5 2.8 psum.7
  343.2 2.3 dynamic-slice_divide_fusion
  (1 shorter events, 0.0 us)
Async XLA Ops:
  6.5 217.4 %all-gather.6.cloned.1.call-start = ((), (), s32[]{:S(2)}) async-start(), calls=%async_computation | async-start | bytes 17039360 | tf_op jit(solution)/shard_map/all_gather | solution.py:14
  7.3 241.6 %all-gather.8.cloned.1.call-start = ((), (), s32[]{:S(2)}) async-start(), calls=%async_computation.1 | async-start | bytes 12582912 | tf_op jit(solution)/shard_map/all_gather | solution.py:8
  8.0 328.0 %all-gather.10.cloned.1.call-start = ((), (), s32[]{:S(2)}) async-start(), calls=%async_computation.2 | async-start | bytes 6291456 | tf_op jit(solution)/shard_map/all_gather | solution.py:26
Sparse Core Ops, SparseCore 0:
  11.1 212.7 all-gather.5
  225.7 23.1 all-gather.7
  273.6 62.3 all-gather.9
